TPU v7x, 512 devices: a whole 4x4x16 slice. The times are simulated.
512 devices in a mesh: tile: 64 (over x, z_lo, core), tm: 8 (over z_hi, y).
Axes of the slice: x: 4, y: 4, z: 16 (z_hi: 2, z_lo: 8; z = z_hi * 8 + z_lo), core: 2. Of those that a mesh axis runs over, the one named last changes fastest.
Arguments:
- controls: float32 [16, 512, 8, 512], P('tm', 'tile'), may hold values from -6 to 6
- perturbations: bfloat16 [8, 16, 4, 512, 8, 512], P('tm', None, None, 'tile'), may hold values from -6 to 6
- owner: int32 [16], replicated, may hold values from 0 to 15, each once
- land_mask: int32 [512, 512], P('tile'), may hold values 0 or 1
- diffusivity: float32 [2, 8], replicated, may hold values from 0.2 to 0.24
Outputs:
- increment: float32 [8, 4, 512, 8, 512], P('tm', None, 'tile')
Inputs may be any that keep to these rules, and one draw needn't show every extreme that they name: owner names every member exactly once.
All inputs are finite; a program needn't handle non-finite values. No bound on the sum of `land_mask` on one device may be relied on, other than what follows from the above.
Results may differ from a plain program's by a relative error of at most 0.0029.
Values may be sent and summed in bfloat16 or wider, within the bound.
A program may use at most 64 MiB of HBM per device.

v0:
```python
import math
import jax
import jax.numpy as jnp
from jax import lax
from jax.sharding import PartitionSpec as P

SWEEPS = 4


def halo_rows(cells, width, dim):
    count = lax.axis_size("tile")
    ends = count - 1
    head = lax.slice_in_dim(cells, 0, width, axis=dim)
    tail = lax.slice_in_dim(cells, cells.shape[dim] - width, cells.shape[dim], axis=dim)
    before = lax.ppermute(tail, "tile", [(i, i + 1) for i in range(ends)])
    after = lax.ppermute(head, "tile", [(i + 1, i) for i in range(ends)])
    return jnp.concatenate([before, cells, after], axis=dim)


def weight_sweep(field, coef):
    padded = jnp.pad(field, ((0, 0), (1, 1), (0, 0), (1, 1)))
    coef_pad = jnp.pad(coef, ((1, 1), (0, 0), (1, 1)))
    flux = 0.5 * (coef + coef_pad[:-2, :, 1:-1]) * (padded[:, :-2, :, 1:-1] - field)
    flux = flux + 0.5 * (coef + coef_pad[2:, :, 1:-1]) * (padded[:, 2:, :, 1:-1] - field)
    flux = flux + 0.5 * (coef + coef_pad[1:-1, :, :-2]) * (padded[:, 1:-1, :, :-2] - field)
    flux = flux + 0.5 * (coef + coef_pad[1:-1, :, 2:]) * (padded[:, 1:-1, :, 2:] - field)
    return field + flux


def on_device(controls, perturbations, owner, land_mask, diffusivity):
    rows = controls.shape[1]
    width = SWEEPS
    tile = lax.axis_index("tile")
    count = lax.axis_size("tile")
    grow = tile * rows - width + jnp.arange(rows + 2 * width)
    inside = (grow >= 0) & (grow < count * rows)
    mask_wide = halo_rows(land_mask, width, 0)
    coef = jnp.where(
        mask_wide[:, None, :] == 1, diffusivity[1][None, :, None], diffusivity[0][None, :, None]
    )
    coef = jnp.where(inside[:, None, None], coef, 0.0)
    keep = inside[None, :, None, None]
    smooth = jnp.where(keep, halo_rows(controls, width, 1), 0.0)
    for sweep_index in range(SWEEPS):
        smooth = jnp.where(keep, weight_sweep(smooth, coef), 0.0)
    weights = smooth[:, width : width + rows].astype(jnp.bfloat16)
    every = lax.all_gather(weights, "tm", axis=0, tiled=True)
    by_member = jnp.zeros_like(every).at[owner].set(every)
    member_count = owner.shape[0]
    factor = 1.0 / math.sqrt(member_count - 1)
    summed = jnp.einsum(
        "mvxly,mxly->vxly", perturbations[0], by_member, preferred_element_type=jnp.float32
    )
    return (summed * factor)[None]


def solution(mesh):
    return jax.shard_map(
        on_device,
        mesh=mesh,
        in_specs=(
            P("tm", "tile", None, None),
            P("tm", None, None, "tile", None, None),
            P(),
            P("tile", None),
            P(),
        ),
        out_specs=P("tm", None, "tile", None, None),
        check_vma=False,
    )
```

profile of v0, /device:TPU:2, one launch (start us, length us, event | category | flops | bytes accessed | tf_op | source)
XLA Modules:
  0.0 150.7 jit_solution(17457148186831489938)
XLA Ops:
  6.5 0.0 all-gather.2.cloned.1.call-start
  6.5 0.8 fusion.59
  7.3 1.9 %collective-permute-start.2 = (s32[4,512]{1,0:T(4,128)S(1)}, s32[4,512]{1,0:T(4,128)S(1)}, u32[]{:S(2)}, u32[]{:S(2)}) collective-permute-start(s32[4,512]{1,0:T(4,128)S(1)} %get-tuple-element.15), channel_id=1, source_target_pairs={{0,8},{8,16},{16,24},{24,32},{32,40},{40,48},{48,56},{56,64},{64,7... | collective-permute-start | bytes 24584 | tf_op jit(solution)/shard_map/ppermute | solution.py:15
  9.3 12.6 %collective-permute-start.3 = (s32[4,512]{1,0:T(4,128)S(1)}, s32[4,512]{1,0:T(4,128)S(1)}, u32[]{:S(2)}, u32[]{:S(2)}) collective-permute-start(s32[4,512]{1,0:T(4,128)S(1)} %get-tuple-element.16), channel_id=1, source_target_pairs={{8,0},{16,8},{24,16},{32,24},{40,32},{48,40},{56,48},{64,56},{72,6... | collective-permute-start | bytes 24584 | tf_op jit(solution)/shard_map/ppermute | solution.py:16
  21.8 1.0 fusion.58
  22.8 1.9 %collective-permute-start = (f32[2,4,8,512]{3,2,1,0:T(8,128)S(1)}, f32[2,4,8,512]{3,2,1,0:T(8,128)S(1)}, u32[]{:S(2)}, u32[]{:S(2)}) collective-permute-start(f32[2,4,8,512]{3,2,1,0:T(8,128)S(1)} %get-tuple-element.13), channel_id=1, source_target_pairs={{0,8},{8,16},{16,24},{24,32},{32,40},{40,48},{48,56},{56,64},{64,7... | collective-permute-start | bytes 393224 | tf_op jit(solution)/shard_map/ppermute | solution.py:15
  24.8 11.1 %collective-permute-start.1 = (f32[2,4,8,512]{3,2,1,0:T(8,128)S(1)}, f32[2,4,8,512]{3,2,1,0:T(8,128)S(1)}, u32[]{:S(2)}, u32[]{:S(2)}) collective-permute-start(f32[2,4,8,512]{3,2,1,0:T(8,128)S(1)} %get-tuple-element.14), channel_id=1, source_target_pairs={{8,0},{16,8},{24,16},{32,24},{40,32},{48,40},{56,48},{64,56},{72,6... | collective-permute-start | bytes 393224 | tf_op jit(solution)/shard_map/ppermute | solution.py:16
  35.9 0.8 slice_bitcast_fusion.1
  36.7 0.1 slice.128
  36.8 0.0 collective-permute-done.2
  36.8 0.0 collective-permute-done.3
  36.8 0.7 add_compare_fusion
  37.5 0.1 select_select_fusion
  37.6 0.2 fusion.45
  37.9 0.0 collective-permute-done
  37.9 0.5 collective-permute-done.1
  38.4 1.0 maximum_select_fusion
  39.5 0.4 fusion.6
  39.9 0.0 copy-start
  39.9 0.4 fusion.19
  40.3 0.4 fusion.32
  40.6 0.3 fusion.40
  41.0 0.8 fusion.56
  41.7 0.0 all-gather.2.cloned.1.call-update
  41.8 0.0 copy-done
  41.8 95.4 %all-gather.2.cloned.1.call-done = bf16[16,8,8,512]{3,2,1,0:T(8,128)(2,1)} async-done(((bf16[2,8,8,512]{3,2,1,0:T(8,128)(2,1)}), bf16[16,8,8,512]{3,2,1,0:T(8,128)(2,1)}) %all-gather.2.cloned.1.call-update) | async-done | bytes 1048592 | tf_op jit(solution)/shard_map/all_gather | solution.py:47
  137.2 0.1 broadcast_in_dim.96
  137.3 2.3 %scatter_fusion = bf16[16,8,8,512]{3,2,1,0:T(8,128)(2,1)S(1)} fusion(bf16[16,8,8,512]{3,2,1,0:T(8,128)(2,1)S(1)} %broadcast_in_dim.96, s32[16]{0:T(128)S(1)} %compare_select_fusion, bf16[16,8,8,512]{3,2,1,0:T(8,128)(2,1)} %all-gather.2.cloned.1.call-done), kind=kCustom, calls=%fused_computation | custom fusion | bytes 3145792 | tf_op jit(solution)/shard_map/scatter | solution.py:48
  139.6 0.3 bitcast_convert_fusion
  139.8 3.2 %multiply_reduce_fusion = f32[8,8,512,4]{2,1,0,3:T(8,128)S(1)} fusion(f32[8,8,512,16]{2,1,0,3:T(8,128)S(1)} %bitcast_convert_fusion, bf16[1,16,4,8,8,512]{5,4,3,2,1,0:T(8,128)(2,1)} %param.6), kind=kLoop, calls=%fused_computation.1 | loop fusion | flops 6160384 | bytes 6815744 | tf_op jit(solution)/shard_map/mvxly,mxly->vxly/dot_general | solution.py:51
  143.0 0.8 multiply_bitcast_fusion
  (4 shorter events, 0.0 us)
Async XLA Ops:
  6.5 130.7 %all-gather.2.cloned.1.call-start = ((), (), s32[]{:S(2)}) async-start(), calls=%async_computation | async-start | bytes 1179648 | tf_op jit(solution)/shard_map/all_gather | solution.py:47
  7.3 29.4 %collective-permute-start.2 = (s32[4,512]{1,0:T(4,128)S(1)}, s32[4,512]{1,0:T(4,128)S(1)}, u32[]{:S(2)}, u32[]{:S(2)}) collective-permute-start(s32[4,512]{1,0:T(4,128)S(1)} %get-tuple-element.15), channel_id=1, source_target_pairs={{0,8},{8,16},{16,24},{24,32},{32,40},{40,48},{48,56},{56,64},{64,7... | collective-permute-start | bytes 24584 | tf_op jit(solution)/shard_map/ppermute | solution.py:15
  9.3 27.5 %collective-permute-start.3 = (s32[4,512]{1,0:T(4,128)S(1)}, s32[4,512]{1,0:T(4,128)S(1)}, u32[]{:S(2)}, u32[]{:S(2)}) collective-permute-start(s32[4,512]{1,0:T(4,128)S(1)} %get-tuple-element.16), channel_id=1, source_target_pairs={{8,0},{16,8},{24,16},{32,24},{40,32},{48,40},{56,48},{64,56},{72,6... | collective-permute-start | bytes 24584 | tf_op jit(solution)/shard_map/ppermute | solution.py:16
  22.8 15.0 %collective-permute-start = (f32[2,4,8,512]{3,2,1,0:T(8,128)S(1)}, f32[2,4,8,512]{3,2,1,0:T(8,128)S(1)}, u32[]{:S(2)}, u32[]{:S(2)}) collective-permute-start(f32[2,4,8,512]{3,2,1,0:T(8,128)S(1)} %get-tuple-element.13), channel_id=1, source_target_pairs={{0,8},{8,16},{16,24},{24,32},{32,40},{40,48},{48,56},{56,64},{64,7... | collective-permute-start | bytes 393224 | tf_op jit(solution)/shard_map/ppermute | solution.py:15
  24.8 13.7 %collective-permute-start.1 = (f32[2,4,8,512]{3,2,1,0:T(8,128)S(1)}, f32[2,4,8,512]{3,2,1,0:T(8,128)S(1)}, u32[]{:S(2)}, u32[]{:S(2)}) collective-permute-start(f32[2,4,8,512]{3,2,1,0:T(8,128)S(1)} %get-tuple-element.14), channel_id=1, source_target_pairs={{8,0},{16,8},{24,16},{32,24},{40,32},{48,40},{56,48},{64,56},{72,6... | collective-permute-start | bytes 393224 | tf_op jit(solution)/shard_map/ppermute | solution.py:16
  39.9 1.9 %copy-start = (s32[16]{0:T(128)S(1)}, s32[16]{0:T(128)}, u32[]{:S(2)}) copy-start(s32[16]{0:T(128)} %param.7) | copy-start | bytes 196
Sparse Core Ops, SparseCore 0:
  41.9 95.2 all-gather.1
where the time goes:
time: 151 us
  waiting for transfers between devices  96 us (64%)
  starting transfers between devices  27.5 us (18%)
  between operations  13.6 us (9%)
  other arithmetic  8.62 us (6%)
  local copies, waits for them, and re-layouts  5.02 us (3%)
    all_gather x1, waiting for transfers between devices, on_device(): every = lax.all_gather(weights, 'tm', axis=0, tiled=True)  95.4 us
    ppermute x2, starting transfers between devices, halo_rows(): after = lax.ppermute(head, 'tile', [(i + 1, i) for i in range(ends)])  23.7 us
    ppermute x2, starting transfers between devices, halo_rows(): before = lax.ppermute(tail, 'tile', [(i, i + 1) for i in range(ends)])  3.83 us
    dot_general x1, other arithmetic, on_device(): jnp.einsum('mvxly,mxly->vxly', perturbations[0], by_member, preferred_ele...  3.17 us
  transfers between devices with their start and end apart: 5, of which 2 were waited for; matrix products, arithmetic and copies ran while one was open for 2% of the time, Pallas kernels for 0%

commit v1 on v0

--- a/solution.py
+++ b/solution.py
@@ -3,8 +3,12 @@
 import jax.numpy as jnp
 from jax import lax
 from jax.sharding import PartitionSpec as P
+from jax.lax import all_to_all, axis_size
 
 SWEEPS = 4
+hold_run_by_axis = lambda arr: jnp.concatenate(
+    all_to_all(jnp.stack(axis_size("tm") * [arr]), "tm", 0, 0), axis=0
+)
 
 
 def halo_rows(cells, width, dim):
@@ -44,7 +48,7 @@
     for sweep_index in range(SWEEPS):
         smooth = jnp.where(keep, weight_sweep(smooth, coef), 0.0)
     weights = smooth[:, width : width + rows].astype(jnp.bfloat16)
-    every = lax.all_gather(weights, "tm", axis=0, tiled=True)
+    every = hold_run_by_axis(weights)
     by_member = jnp.zeros_like(every).at[owner].set(every)
     member_count = owner.shape[0]
     factor = 1.0 / math.sqrt(member_count - 1)

time: 151 us -> 101 us (0.67)
  the two profiles are of different devices: /device:TPU:2 before, /device:TPU:101 now
where the time goes in v1:
time: 101 us
  waiting for transfers between devices  60.9 us (60%)
  starting transfers between devices  26.6 us (26%)
  other arithmetic  7.98 us (8%)
  local copies, waits for them, and re-layouts  4.95 us (5%)
    all_to_all x1, waiting for transfers between devices, all_to_all(jnp.stack(axis_size('tm') * [arr]), 'tm', 0, 0)  57.2 us
    all_to_all x1, starting transfers between devices, all_to_all(jnp.stack(axis_size('tm') * [arr]), 'tm', 0, 0)  12.6 us
    ppermute x2, starting transfers between devices, halo_rows(): before = lax.ppermute(tail, 'tile', [(i, i + 1) for i in range(ends)])  10.2 us
    ppermute x2, starting transfers between devices, halo_rows(): after = lax.ppermute(head, 'tile', [(i + 1, i) for i in range(ends)])  3.84 us
    ppermute x2, waiting for transfers between devices, halo_rows(): after = lax.ppermute(head, 'tile', [(i + 1, i) for i in range(ends)])  3.62 us
    dot_general x1, other arithmetic, on_device(): jnp.einsum('mvxly,mxly->vxly', perturbations[0], by_member, preferred_ele...  3.17 us
  transfers between devices with their start and end apart: 5, of which 2 were waited for; matrix products, arithmetic and copies ran while one was open for 3% of the time, Pallas kernels for 0%

profile of v1, /device:TPU:101, one launch (start us, length us, event | category | flops | bytes accessed | tf_op | source)
XLA Modules:
  0.0 100.6 jit_solution(18037231514869602997)
XLA Ops:
  0.0 0.8 fusion.59
  0.8 5.3 %collective-permute-start.2 = (s32[4,512]{1,0:T(4,128)S(1)}, s32[4,512]{1,0:T(4,128)S(1)}, u32[]{:S(2)}, u32[]{:S(2)}) collective-permute-start(s32[4,512]{1,0:T(4,128)S(1)} %get-tuple-element.15), channel_id=1, source_target_pairs={{0,8},{8,16},{16,24},{24,32},{32,40},{40,48},{48,56},{56,64},{64,7... | collective-permute-start | bytes 24584 | tf_op jit(solution)/shard_map/ppermute | solution.py:19
  6.1 1.9 %collective-permute-start.3 = (s32[4,512]{1,0:T(4,128)S(1)}, s32[4,512]{1,0:T(4,128)S(1)}, u32[]{:S(2)}, u32[]{:S(2)}) collective-permute-start(s32[4,512]{1,0:T(4,128)S(1)} %get-tuple-element.16), channel_id=1, source_target_pairs={{8,0},{16,8},{24,16},{32,24},{40,32},{48,40},{56,48},{64,56},{72,6... | collective-permute-start | bytes 24584 | tf_op jit(solution)/shard_map/ppermute | solution.py:20
  8.0 1.0 fusion.58
  9.0 4.9 %collective-permute-start = (f32[2,4,8,512]{3,2,1,0:T(8,128)S(1)}, f32[2,4,8,512]{3,2,1,0:T(8,128)S(1)}, u32[]{:S(2)}, u32[]{:S(2)}) collective-permute-start(f32[2,4,8,512]{3,2,1,0:T(8,128)S(1)} %get-tuple-element.13), channel_id=1, source_target_pairs={{0,8},{8,16},{16,24},{24,32},{32,40},{40,48},{48,56},{56,64},{64,7... | collective-permute-start | bytes 393224 | tf_op jit(solution)/shard_map/ppermute | solution.py:19
  13.9 1.9 %collective-permute-start.1 = (f32[2,4,8,512]{3,2,1,0:T(8,128)S(1)}, f32[2,4,8,512]{3,2,1,0:T(8,128)S(1)}, u32[]{:S(2)}, u32[]{:S(2)}) collective-permute-start(f32[2,4,8,512]{3,2,1,0:T(8,128)S(1)} %get-tuple-element.14), channel_id=1, source_target_pairs={{8,0},{16,8},{24,16},{32,24},{40,32},{48,40},{56,48},{64,56},{72,6... | collective-permute-start | bytes 393224 | tf_op jit(solution)/shard_map/ppermute | solution.py:20
  15.8 0.8 slice_bitcast_fusion.1
  16.6 0.1 slice.128
  16.7 0.0 collective-permute-done.2
  16.7 0.0 collective-permute-done.3
  16.7 0.7 add_compare_fusion
  17.4 0.1 select_select_fusion
  17.5 0.2 fusion.45
  17.8 0.0 collective-permute-done
  17.8 3.6 %collective-permute-done.1 = f32[2,4,8,512]{3,2,1,0:T(8,128)S(1)} collective-permute-done((f32[2,4,8,512]{3,2,1,0:T(8,128)S(1)}, f32[2,4,8,512]{3,2,1,0:T(8,128)S(1)}, u32[]{:S(2)}, u32[]{:S(2)}) %collective-permute-start.1) | collective-permute-done | bytes 131104 | tf_op jit(solution)/shard_map/ppermute | solution.py:20
  21.4 1.0 %maximum_select_fusion = f32[2,16,8,512]{3,2,1,0:T(8,128)S(1)} fusion(f32[2,4,8,512]{3,2,1,0:T(8,128)S(1)} %collective-permute-done.1, f32[2,8,8,512]{3,2,1,0:T(8,128)} %param.5, f32[2,4,8,512]{3,2,1,0:T(8,128)S(1)} %collective-permute-done, pred[16]{0:T(512)(128)(4,1)S(1)} %compare_and_fusion), kind=kLoop, calls=%fused_computation.63 | loop fusion | flops 393216 | bytes 1048592 | tf_op jit(solution)/shard_map/jit(_where)/select_n | solution.py:47
  22.5 0.4 fusion.6
  22.8 0.4 fusion.19
  23.2 0.4 fusion.32
  23.6 0.0 copy-start
  23.6 0.3 fusion.40
  24.0 0.1 fusion.56
  24.1 1.1 %stack.2 = bf16[8,2,8,8,512]{4,3,2,1,0:T(8,128)(2,1)} broadcast(bf16[2,8,8,512]{3,2,1,0:T(8,128)(2,1)S(1)} %fusion.56), dimensions={1,2,3,4} | broadcast | bytes 1179648 | tf_op jit(solution)/shard_map/stack | solution.py:10
  25.2 12.6 %all-to-all-start = ((bf16[8,2,8,8,512]{4,3,2,1,0:T(8,128)(2,1)}), bf16[8,2,8,8,512]{4,3,2,1,0:T(8,128)(2,1)S(1)}, u32[]{:S(2)}, u32[]{:S(2)}) async-start(bf16[8,2,8,8,512]{4,3,2,1,0:T(8,128)(2,1)} %stack.2), calls=%async_computation | async-start | bytes 2097152 | tf_op jit(solution)/shard_map/all_to_all | solution.py:10
  37.8 0.0 copy-done
  37.8 57.2 %all-to-all-done = bf16[8,2,8,8,512]{4,3,2,1,0:T(8,128)(2,1)S(1)} async-done(((bf16[8,2,8,8,512]{4,3,2,1,0:T(8,128)(2,1)}), bf16[8,2,8,8,512]{4,3,2,1,0:T(8,128)(2,1)S(1)}, u32[]{:S(2)}, u32[]{:S(2)}) %all-to-all-start) | async-done | bytes 1048608 | tf_op jit(solution)/shard_map/all_to_all | solution.py:10
  95.1 0.1 broadcast_in_dim.96
  95.2 1.1 %scatter_fusion = bf16[16,8,8,512]{3,2,1,0:T(8,128)(2,1)S(1)} fusion(bf16[16,8,8,512]{3,2,1,0:T(8,128)(2,1)S(1)} %broadcast_in_dim.96, s32[16]{0:T(128)S(1)} %compare_select_fusion, bf16[16,8,8,512]{3,2,1,0:T(8,128)(2,1)S(1)} %bitcast.15), kind=kCustom, calls=%fused_computation | custom fusion | bytes 3145792 | tf_op jit(solution)/shard_map/scatter | solution.py:52
  96.3 0.3 bitcast_convert_fusion
  96.6 3.2 %multiply_reduce_fusion = f32[8,8,512,4]{2,1,0,3:T(8,128)S(1)} fusion(f32[8,8,512,16]{2,1,0,3:T(8,128)S(1)} %bitcast_convert_fusion, bf16[1,16,4,8,8,512]{5,4,3,2,1,0:T(8,128)(2,1)} %param.6), kind=kLoop, calls=%fused_computation.1 | loop fusion | flops 6160384 | bytes 6815744 | tf_op jit(solution)/shard_map/mvxly,mxly->vxly/dot_general | solution.py:55
  99.8 0.8 multiply_bitcast_fusion
  (4 shorter events, 0.0 us)
Async XLA Ops:
  0.8 15.9 %collective-permute-start.2 = (s32[4,512]{1,0:T(4,128)S(1)}, s32[4,512]{1,0:T(4,128)S(1)}, u32[]{:S(2)}, u32[]{:S(2)}) collective-permute-start(s32[4,512]{1,0:T(4,128)S(1)} %get-tuple-element.15), channel_id=1, source_target_pairs={{0,8},{8,16},{16,24},{24,32},{32,40},{40,48},{48,56},{56,64},{64,7... | collective-permute-start | bytes 24584 | tf_op jit(solution)/shard_map/ppermute | solution.py:19
  6.1 10.6 %collective-permute-start.3 = (s32[4,512]{1,0:T(4,128)S(1)}, s32[4,512]{1,0:T(4,128)S(1)}, u32[]{:S(2)}, u32[]{:S(2)}) collective-permute-start(s32[4,512]{1,0:T(4,128)S(1)} %get-tuple-element.16), channel_id=1, source_target_pairs={{8,0},{16,8},{24,16},{32,24},{40,32},{48,40},{56,48},{64,56},{72,6... | collective-permute-start | bytes 24584 | tf_op jit(solution)/shard_map/ppermute | solution.py:20
  9.0 8.7 %collective-permute-start = (f32[2,4,8,512]{3,2,1,0:T(8,128)S(1)}, f32[2,4,8,512]{3,2,1,0:T(8,128)S(1)}, u32[]{:S(2)}, u32[]{:S(2)}) collective-permute-start(f32[2,4,8,512]{3,2,1,0:T(8,128)S(1)} %get-tuple-element.13), channel_id=1, source_target_pairs={{0,8},{8,16},{16,24},{24,32},{32,40},{40,48},{48,56},{56,64},{64,7... | collective-permute-start | bytes 393224 | tf_op jit(solution)/shard_map/ppermute | solution.py:19
  13.9 7.5 %collective-permute-start.1 = (f32[2,4,8,512]{3,2,1,0:T(8,128)S(1)}, f32[2,4,8,512]{3,2,1,0:T(8,128)S(1)}, u32[]{:S(2)}, u32[]{:S(2)}) collective-permute-start(f32[2,4,8,512]{3,2,1,0:T(8,128)S(1)} %get-tuple-element.14), channel_id=1, source_target_pairs={{8,0},{16,8},{24,16},{32,24},{40,32},{48,40},{56,48},{64,56},{72,6... | collective-permute-start | bytes 393224 | tf_op jit(solution)/shard_map/ppermute | solution.py:20
  23.6 14.2 %copy-start = (s32[16]{0:T(128)S(1)}, s32[16]{0:T(128)}, u32[]{:S(2)}) copy-start(s32[16]{0:T(128)} %param.7) | copy-start | bytes 196
  25.2 69.9 %all-to-all-start = ((bf16[8,2,8,8,512]{4,3,2,1,0:T(8,128)(2,1)}), bf16[8,2,8,8,512]{4,3,2,1,0:T(8,128)(2,1)S(1)}, u32[]{:S(2)}, u32[]{:S(2)}) async-start(bf16[8,2,8,8,512]{4,3,2,1,0:T(8,128)(2,1)} %stack.2), calls=%async_computation | async-start | bytes 2097152 | tf_op jit(solution)/shard_map/all_to_all | solution.py:10
